TPU v7x, 128 devices: a whole 4x4x4 slice. The times are simulated.
128 devices in a mesh: dp: 32 (over x, z, core), enc: 4 (over y).
Axes of the slice: x: 4, y: 4, z: 4, core: 2. Of those that a mesh axis runs over, the one named last changes fastest.
Arguments:
- hidden: bfloat16 [16384, 4096], P('dp', 'enc'), may hold values from -6 to 6
- norm_gain: float32 [4096], replicated, may hold values from 0.25 to 1.75
- w_query: bfloat16 [4096, 2048], P('dp', 'enc'), may hold values from -0.09375 to 0.09375
- w_key: bfloat16 [896, 2048], P('dp', 'enc'), may hold values from -0.1875 to 0.1875
- w_value: bfloat16 [896, 2048], P('dp', 'enc'), may hold values from -0.1875 to 0.1875
- w_out: bfloat16 [2048, 4096], P('enc', 'dp'), may hold values from -0.125 to 0.125
- w_cond: bfloat16 [4096, 896], P('dp', 'enc'), may hold values from -0.75 to 0.75
- enc_gain: float32 [896], replicated, may hold values from 0.25 to 1.75
- store: bfloat16 [1024, 128, 896], P(('dp', 'enc')), may hold values from -6 to 6
- neighbour_ids: int32 [512], P(('dp', 'enc')), may hold values from 0 to 1023, as said below
- out_grad: bfloat16 [16384, 4096], P('dp', 'enc'), may hold values from -6 to 6
Outputs:
- layer_out: bfloat16 [16384, 4096], P('dp', 'enc')
- hidden_grad: float32 [16384, 4096], P('dp', 'enc')
- query_grad: float32 [4096, 2048], P('dp', 'enc')
- key_grad: float32 [896, 2048], P('dp', 'enc')
- value_grad: float32 [896, 2048], P('dp', 'enc')
- out_weight_grad: float32 [2048, 4096], P('enc', 'dp')
- cond_grad: float32 [4096, 896], P('dp', 'enc')
Inputs may be any that keep to these rules, and one draw needn't show every extreme that they name: `neighbour_ids`: slot n names a neighbour stored on a device of the same data index as the device holding slot n (device k holds rows k * 8 to (k + 1) * 8 - 1). Among the 4 slots of one device at most 2 name rows of one device, and for every data index one device is named by exactly 2 slots of each of the 4 devices.
All inputs are finite; a program needn't handle non-finite values.
Results may differ from a plain program's by a relative error of at most 0.019.
Values may be sent and summed in bfloat16 or wider, within the bound.
A program may use at most 192 MiB of HBM per device.

v0:
```python
import jax
import jax.numpy as jnp
from jax import lax
from jax.sharding import PartitionSpec as P

HSZ = 128
SPAN = 64
NBR = 2
NL = 128
epsilon = 1e-05


def side_by_side(arrays, axis, dim, along):
    ends, at = ([], 0)
    for a in arrays[:-1]:
        at += a.shape[along]
        ends.append(at)
    both = jnp.concatenate(arrays, axis=along)
    return tuple(jnp.split(lax.all_gather(both, axis, axis=dim, tiled=True), ends, axis=along))


def joined_along(tiles, dim):
    tiles = jnp.moveaxis(tiles, 0, dim)
    dims = tiles.shape
    return tiles.reshape(*dims[:dim], dims[dim] * dims[dim + 1], *dims[dim + 2 :])


def copy_for_each(shard, axis):
    copies = jnp.broadcast_to(shard, (lax.axis_size(axis), *shard.shape))
    return lax.all_to_all(copies, axis, split_axis=0, concat_axis=0, tiled=True)


def collect(shard, axis, dim):
    return joined_along(copy_for_each(shard, axis), dim)


def in_blocks(shard, dim, peers):
    dims = shard.shape
    tiles = shard.reshape(*dims[:dim], peers, dims[dim] // peers, *dims[dim + 1 :])
    return jnp.moveaxis(tiles, dim, 0)


def summed_on_arrival(shard, axis, dim):
    peers = lax.axis_size(axis)
    tiles = lax.all_to_all(in_blocks(shard, dim, peers), axis, 0, 0, tiled=True)
    return jnp.sum(tiles.astype(jnp.float32), axis=0)


def one_scatter(arrays, axis, dims):
    peers = lax.axis_size(axis)
    tiles = [in_blocks(a, dim, peers) for a, dim in zip(arrays, dims)]
    lines = jnp.concatenate([b.reshape(peers, -1) for b in tiles], axis=1)
    extent = max(16, -(-lines.shape[1] // 1024) * 8)
    lines = jnp.pad(lines, ((0, 0), (0, extent * 128 - lines.shape[1]))).reshape(-1, 128)
    flat, at, done = (lax.psum_scatter(lines, axis, tiled=True).reshape(-1), 0, [])
    for b in tiles:
        part = b[0]
        done.append(flat[at : at + part.size].reshape(part.shape))
        at += part.size
    return tuple(done)


def rms_scale(values):
    return lax.rsqrt(jnp.mean(values * values, axis=-1, keepdims=True) + epsilon)


def encoder_input(raw_rows, cond_rows):
    enc_in = raw_rows.astype(jnp.float32) + cond_rows.astype(jnp.float32)[..., None, :]
    return (enc_in, rms_scale(enc_in))


def encode_rows(raw_rows, cond_rows, enc_gain):
    enc_in, enc_rstd = encoder_input(raw_rows, cond_rows)
    return (enc_in * enc_rstd * enc_gain).astype(jnp.bfloat16)


def cond_gradient(raw_rows, cond_rows, enc_gain, grad_rows):
    enc_in, enc_rstd = encoder_input(raw_rows, cond_rows)
    scaled_enc = enc_gain * grad_rows.astype(jnp.float32)
    enc_mean = jnp.mean(enc_in * scaled_enc, axis=-1, keepdims=True)
    return jnp.sum(enc_rstd * scaled_enc - enc_in * enc_rstd**3 * enc_mean, axis=-2)


def contract_first(left, right):
    return lax.dot_general(
        left, right, (((0,), (0,)), ((), ())), preferred_element_type=jnp.float32
    )


def contract_last(left, right):
    return lax.dot_general(
        left, right, (((1,), (1,)), ((), ())), preferred_element_type=jnp.float32
    )


def shards(
    hidden,
    norm_gain,
    w_query,
    w_key,
    w_value,
    w_out,
    w_cond,
    enc_gain,
    store,
    neighbour_ids,
    out_grad,
):
    groups = lax.axis_size("enc")
    member = lax.axis_index("enc")
    tok_rows = hidden.shape[0]
    feature_cols = hidden.shape[1]
    model_width = feature_cols * groups
    head_cols = w_query.shape[1]
    enc_width = w_key.shape[0] * lax.axis_size("dp")
    enc_cols = w_cond.shape[1]
    span_count = tok_rows // SPAN
    requests = neighbour_ids.shape[0]
    capacity = max(2, (requests + 1) // 2)
    store_rows = store.shape[0]
    heads_here = head_cols // HSZ
    keys_len = NBR * NL
    score_scale = HSZ ** (-0.5)
    full_rows = lax.all_gather(hidden, "enc", axis=1, tiled=True)
    inputs = full_rows.astype(jnp.float32)
    row_rstd = rms_scale(inputs)
    normed = (inputs * row_rstd * norm_gain).astype(jnp.bfloat16)
    w_query_all, w_key_all, w_value_all, w_cond_all = (
        lax.all_gather(w_query, "dp", axis=0, tiled=True),
        *side_by_side((w_key, w_value), "dp", 0, 1),
        lax.all_gather(w_cond, "dp", axis=0, tiled=True),
    )
    queries = jnp.dot(normed, w_query_all, preferred_element_type=jnp.float32).astype(jnp.bfloat16)
    w_out_all = lax.all_gather(w_out, "dp", axis=1, tiled=True)
    summary = jnp.mean(inputs.reshape(span_count, SPAN, model_width), axis=1).astype(jnp.bfloat16)
    cond_part = jnp.dot(summary, w_cond_all, preferred_element_type=jnp.float32).astype(
        jnp.bfloat16
    )
    condition = collect(cond_part, "enc", 1)
    request_order = jnp.arange(requests)
    my_spans = (member * requests + request_order) // NBR
    cond_req = jnp.take(condition, my_spans, axis=0)
    owner_of = neighbour_ids // store_rows % groups
    store_row = neighbour_ids % store_rows
    earlier = (owner_of[:, None] == owner_of[None, :]) & (
        request_order[None, :] < request_order[:, None]
    )
    slot_rank = jnp.sum(earlier.astype(jnp.int32), axis=1)
    slot_index = owner_of * capacity + slot_rank
    selection = slot_index[None, :] == jnp.arange(groups * capacity)[:, None]
    row_buffer = jnp.sum(jnp.where(selection, store_row[None, :], 0), axis=1).reshape(
        groups, capacity
    )
    raw_buffer = lax.all_to_all(
        jnp.take(
            store,
            lax.all_to_all(row_buffer, "enc", split_axis=0, concat_axis=0, tiled=True),
            axis=0,
        ),
        "enc",
        split_axis=0,
        concat_axis=0,
        tiled=True,
    )
    raw_mine = jnp.take(raw_buffer.reshape(groups * capacity, NL, enc_width), slot_index, axis=0)
    encoded_mine = encode_rows(raw_mine, cond_req, enc_gain)
    encoded = lax.all_gather(encoded_mine, "enc", axis=0, tiled=True)
    flat_enc = encoded.reshape(-1, enc_width)
    keys_proj = jnp.dot(flat_enc, w_key_all, preferred_element_type=jnp.float32).astype(
        jnp.bfloat16
    )
    values_proj = jnp.dot(flat_enc, w_value_all, preferred_element_type=jnp.float32).astype(
        jnp.bfloat16
    )
    query_heads = queries.reshape(span_count, SPAN, heads_here, HSZ)
    key_heads = keys_proj.reshape(span_count, keys_len, heads_here, HSZ)
    value_heads = values_proj.reshape(span_count, keys_len, heads_here, HSZ)
    scores = (
        jnp.einsum("cqhd,ckhd->chqk", query_heads, key_heads, preferred_element_type=jnp.float32)
        * score_scale
    )
    attn_full = jax.nn.softmax(scores, axis=-1)
    attn_weights = attn_full.astype(jnp.bfloat16)
    attended = (
        jnp.einsum("chqk,ckhd->cqhd", attn_weights, value_heads, preferred_element_type=jnp.float32)
        .astype(jnp.bfloat16)
        .reshape(tok_rows, head_cols)
    )
    out_term = jnp.dot(attended, w_out_all, preferred_element_type=jnp.float32)
    projected = summed_on_arrival(out_term.astype(jnp.bfloat16), "enc", 1)
    layer_out = (hidden.astype(jnp.float32) + projected).astype(jnp.bfloat16)
    grad_rows = lax.all_gather(out_grad, "enc", axis=1, tiled=True)
    attended_grad = contract_last(grad_rows, w_out_all).astype(jnp.bfloat16)
    out_weight_grad = lax.psum_scatter(
        contract_first(attended, grad_rows).astype(jnp.bfloat16),
        "dp",
        scatter_dimension=1,
        tiled=True,
    ).astype(jnp.float32)
    grad_heads = attended_grad.reshape(span_count, SPAN, heads_here, HSZ)
    prob_grad = jnp.einsum(
        "cqhd,ckhd->chqk", grad_heads, value_heads, preferred_element_type=jnp.float32
    )
    score_grad = (
        attn_full
        * (prob_grad - jnp.sum(attn_full * prob_grad, axis=-1, keepdims=True))
        * score_scale
    ).astype(jnp.bfloat16)
    query_act_grad = (
        jnp.einsum("chqk,ckhd->cqhd", score_grad, key_heads, preferred_element_type=jnp.float32)
        .astype(jnp.bfloat16)
        .reshape(tok_rows, head_cols)
    )
    key_act_grad = (
        jnp.einsum("chqk,cqhd->ckhd", score_grad, query_heads, preferred_element_type=jnp.float32)
        .astype(jnp.bfloat16)
        .reshape(-1, head_cols)
    )
    value_act_grad = (
        jnp.einsum("chqk,cqhd->ckhd", attn_weights, grad_heads, preferred_element_type=jnp.float32)
        .astype(jnp.bfloat16)
        .reshape(-1, head_cols)
    )
    query_grad = lax.psum_scatter(
        contract_first(normed, query_act_grad).astype(jnp.bfloat16),
        "dp",
        scatter_dimension=0,
        tiled=True,
    ).astype(jnp.float32)
    enc_term = contract_last(key_act_grad, w_key_all) + contract_last(value_act_grad, w_value_all)
    encoded_grad = (
        summed_on_arrival(enc_term.astype(jnp.bfloat16), "enc", 0)
        .astype(jnp.bfloat16)
        .reshape(requests, NL, enc_width)
    )
    cond_mine = cond_gradient(raw_mine, cond_req, enc_gain, encoded_grad)
    slot_grads = collect(cond_mine, "enc", 0)
    cond_delta = jnp.sum(slot_grads.reshape(span_count, NBR, enc_width), axis=1).astype(
        jnp.bfloat16
    )
    delta_cols = lax.dynamic_slice_in_dim(cond_delta, member * enc_cols, enc_cols, 1)
    key_term = contract_first(flat_enc, key_act_grad)
    value_term = contract_first(flat_enc, value_act_grad)
    cond_term = contract_first(summary, delta_cols)
    key_grad, value_grad, cond_grad = tuple(
        (
            part.astype(jnp.float32)
            for part in one_scatter(
                (
                    key_term.astype(jnp.bfloat16),
                    value_term.astype(jnp.bfloat16),
                    cond_term.astype(jnp.bfloat16),
                ),
                "dp",
                (0, 0, 0),
            )
        )
    )
    summary_term = contract_last(delta_cols, w_cond_all)
    normed_term = contract_last(query_act_grad, w_query_all)
    normed_grad, summary_grad = (
        lax.psum(normed_term.astype(jnp.bfloat16), "enc").astype(jnp.float32),
        lax.psum(summary_term.astype(jnp.bfloat16), "enc").astype(jnp.float32),
    )
    scaled = normed_grad * norm_gain
    row_mean = jnp.mean(inputs * scaled, axis=-1, keepdims=True)
    full_grad = (
        grad_rows.astype(jnp.float32)
        + (row_rstd * scaled - inputs * row_rstd**3 * row_mean)
        + jnp.repeat(summary_grad / SPAN, SPAN, axis=0)
    )
    hidden_grad = lax.dynamic_slice_in_dim(full_grad, member * feature_cols, feature_cols, 1)
    return (layer_out, hidden_grad, query_grad, key_grad, value_grad, out_weight_grad, cond_grad)


def solution(mesh):
    placed = (
        P("dp", "enc"),
        P(),
        P("dp", "enc"),
        P("dp", "enc"),
        P("dp", "enc"),
        P("enc", "dp"),
        P("dp", "enc"),
        P(),
        P(("dp", "enc"), None, None),
        P(("dp", "enc")),
        P("dp", "enc"),
    )
    return jax.shard_map(
        shards,
        mesh=mesh,
        in_specs=placed,
        out_specs=(
            P("dp", "enc"),
            P("dp", "enc"),
            P("dp", "enc"),
            P("dp", "enc"),
            P("dp", "enc"),
            P("enc", "dp"),
            P("dp", "enc"),
        ),
        check_vma=False,
    )
```

profile of v0, /device:TPU:0, one launch (start us, length us, event | category | flops | bytes accessed | tf_op | source)
XLA Modules:
  0.0 741.9 jit_solution(10964547584921568469)
XLA Ops:
  11.8 9.6 %all_to_all.40 = s32[4,1,2]{2,1,0:T(1,128)S(1)} all-to-all(s32[4,1,2]{2,1,0:T(1,128)S(1)} %bitcast.99), channel_id=1, replica_groups=mesh['dp'=32,'enc'=4] {'enc'}, dimensions={0} | all-to-all | bytes 64 | tf_op jit(solution)/shard_map/all_to_all | solution.py:157
  23.8 3.1 broadcast_select_fusion
  26.9 3.6 all-to-all-start.1
  30.6 49.5 %all-gather.9.cloned.1.call-done = bf16[512,4096]{1,0:T(8,128)(2,1)} async-done(((bf16[512,1024]{1,0:T(8,128)(2,1)}), bf16[512,4096]{1,0:T(8,128)(2,1)}) %all-gather.9.cloned.1.call-update) | async-done | bytes 4194320 | tf_op jit(solution)/shard_map/all_gather | solution.py:124
  80.1 3.0 bitcast_reduce_fusion
  83.1 43.9 %all-gather.11.cloned.1.call-done = bf16[4096,224]{0,1:T(8,128)(2,1)} async-done(((bf16[128,224]{0,1:T(8,128)(2,1)}), bf16[4096,224]{0,1:T(8,128)(2,1)}) %all-gather.11.cloned.1.call-update) | async-done | bytes 1835024 | tf_op jit(solution)/shard_map/all_gather | solution.py:131
  129.8 4.3 all-to-all-start.2
  136.4 3.1 all-to-all-done.2
  144.0 29.2 %all-gather.21.cloned.1.call-done = bf16[32,28,1024]{2,1,0:T(8,128)(2,1)} async-done(((bf16[1,28,1024]{2,1,0:T(8,128)(2,1)}), bf16[32,28,1024]{2,1,0:T(8,128)(2,1)}) %all-gather.21.cloned.1.call-update) | async-done | bytes 1835024 | tf_op jit(solution)/shard_map/all_gather | solution.py:19
  173.2 3.7 reshape.330
  177.0 3.1 multiply_reduce_fusion.1
  180.6 40.4 %all-gather.15.cloned.1.call-done = bf16[4096,512]{1,0:T(8,128)(2,1)} async-done(((bf16[128,512]{1,0:T(8,128)(2,1)}), bf16[4096,512]{1,0:T(8,128)(2,1)}) %all-gather.15.cloned.1.call-update) | async-done | bytes 4194320 | tf_op jit(solution)/shard_map/all_gather | solution.py:129
  221.0 5.8 convolution_convert_fusion.11
  227.0 39.4 %all-gather.13.cloned.1.call-done = bf16[16,128,896]{2,1,0:T(8,128)(2,1)} async-done(((bf16[4,128,896]{2,1,0:T(8,128)(2,1)}), bf16[16,128,896]{2,1,0:T(8,128)(2,1)}) %all-gather.13.cloned.1.call-update) | async-done | bytes 3670032 | tf_op jit(solution)/shard_map/all_gather | solution.py:167
  266.4 5.9 convolution_convert_fusion.6
  272.3 4.0 reshape.289
  276.3 6.4 convolution_convert_fusion.7
  282.7 4.2 reshape.287
  291.4 6.0 fusion.34
  297.7 18.7 %all-gather.19.cloned.1.call-done = bf16[512,4096]{1,0:T(8,128)(2,1)} async-done(((bf16[512,1024]{1,0:T(8,128)(2,1)}), bf16[512,4096]{1,0:T(8,128)(2,1)}) %all-gather.19.cloned.1.call-update) | async-done | bytes 4194320 | tf_op jit(solution)/shard_map/all_gather | solution.py:192
  316.4 6.5 convolution_convert_fusion
  323.0 6.5 copy.112
  329.9 38.4 %all-gather.17.cloned.1.call-done = bf16[512,4096]{1,0:T(8,128)(2,1)} async-done(((bf16[512,128]{1,0:T(8,128)(2,1)}), bf16[512,4096]{1,0:T(8,128)(2,1)}) %all-gather.17.cloned.1.call-update) | async-done | bytes 4194320 | tf_op jit(solution)/shard_map/all_gather | solution.py:134
  368.4 5.8 convolution_convert_fusion.10
  374.3 3.8 fusion.9
  378.1 16.3 %fusion.37 = bf16[8,64,4,128]{3,1,2,0:T(8,128)(2,1)} fusion(bf16[8,256,4,128]{3,2,1,0:T(4,128)(2,1)} %reshape.289, f32[8,4,64,256]{3,2,1,0:T(8,128)} %fusion.9, f32[8,4,64,256]{3,2,1,0:T(8,128)} %get-tuple-element.50, f32[8,4,64]{2,1,0:T(4,128)S(1)} %get-tuple-element.49), kind=kOutput, calls=%fused_computation.62 | convolution fusion | flops 138152192 | bytes 6823936 | tf_op jit(solution)/shard_map/chqk,ckhd->cqhd/dot_general | solution.py:210
  395.9 6.8 convolution_convert_fusion.1
  402.7 16.7 %convert_bitcast_fusion.1 = bf16[8,256,4,128]{1,3,2,0:T(8,128)(2,1)} fusion(f32[8,4,64,256]{3,2,1,0:T(8,128)} %fusion.9, bf16[8,64,4,128]{3,2,1,0:T(4,128)(2,1)S(1)} %reshape.288, f32[8,4,64,256]{3,2,1,0:T(8,128)} %get-tuple-element.50, f32[8,4,64]{2,1,0:T(4,128)S(1)} %get-tuple-element.49), kind=kOutput, calls=%fused_computation.29 | convolution fusion | flops 138938624 | bytes 6823936 | tf_op jit(solution)/shard_map/chqk,cqhd->ckhd/dot_general | solution.py:215
  424.4 7.0 convert_bitcast_fusion
  439.5 4.4 add_convert_fusion
  443.9 5.0 all-to-all-start.4
  448.9 6.7 convolution_convert_fusion.2
  455.7 3.0 convolution_convert_fusion.8
  458.7 3.0 convolution_convert_fusion.9
  461.8 31.0 %all-to-all-done.4 = bf16[4,512,896]{2,1,0:T(8,128)(2,1)} async-done(((bf16[4,512,896]{2,1,0:T(8,128)(2,1)}), bf16[4,512,896]{2,1,0:T(8,128)(2,1)}, u32[]{:S(2)}, u32[]{:S(2)}) %all-to-all-start.4) | async-done | bytes 3670048 | tf_op jit(solution)/shard_map/all_to_all | solution.py:45
  492.8 3.1 reduce_sum.133
  497.9 3.5 all-to-all-start.5
  501.4 4.8 convolution_convert_fusion.3
  511.8 4.9 all-to-all-start.3
  520.1 5.0 reshape_reshape.15
  531.0 5.2 reshape.298
  536.3 6.5 convert_element_type.163
  542.8 36.6 %all-to-all-done.3 = bf16[4,512,1024]{2,1,0:T(8,128)(2,1)} async-done(((bf16[4,512,1024]{2,1,0:T(8,128)(2,1)}), bf16[4,512,1024]{2,1,0:T(8,128)(2,1)}, u32[]{:S(2)}, u32[]{:S(2)}) %all-to-all-start.3) | async-done | bytes 4194336 | tf_op jit(solution)/shard_map/all_to_all | solution.py:45
  579.4 3.5 convert_reduce_fusion
  587.7 58.2 %all-reduce.3.cloned.1.call-done = (bf16[8,4096]{1,0:T(8,128)(2,1)}, bf16[512,4096]{1,0:T(8,128)(2,1)}) async-done(((bf16[8,4096]{1,0:T(8,128)(2,1)}, bf16[512,4096]{1,0:T(8,128)(2,1)}), (bf16[8,4096]{1,0:T(8,128)(2,1)}, bf16[512,4096]{1,0:T(8,128)(2,1)})) %all-reduce.3.cloned.1.call-update) | async-done | bytes 4259856 | tf_op jit(solution)/shard_map/psum | solution.py:263
  645.9 4.9 multiply_reduce_fusion
  651.9 4.0 dynamic-slice_add_fusion
  655.9 75.2 %reduce-scatter.8.cloned.1.call-done = bf16[448,128]{1,0:T(8,128)(2,1)} async-done(((bf16[14336,128]{1,0:T(8,128)(2,1)}), bf16[448,128]{1,0:T(8,128)(2,1)}) %reduce-scatter.8.cloned.1.call-update) | async-done | bytes 114704 | tf_op jit(solution)/shard_map/reduce_scatter | solution.py:55
  (145 shorter events, 63.5 us)
Async XLA Ops:
  7.2 14.6 %copy-start = (bf16[8,128,896]{2,1,0:T(8,128)(2,1)S(1)}, bf16[8,128,896]{2,1,0:T(8,128)(2,1)}, u32[]{:S(2)}) copy-start(bf16[8,128,896]{2,1,0:T(8,128)(2,1)} %param.19) | copy-start | bytes 5505028
  7.2 72.9 %all-gather.9.cloned.1.call-start = ((), (), s32[]{:S(2)}) async-start(), calls=%async_computation.9 | async-start | bytes 5242880 | tf_op jit(solution)/shard_map/all_gather | solution.py:124
  7.9 119.2 %all-gather.11.cloned.1.call-start = ((), (), s32[]{:S(2)}) async-start(), calls=%async_computation.10 | async-start | bytes 1892352 | tf_op jit(solution)/shard_map/all_gather | solution.py:131
  8.7 164.6 %all-gather.21.cloned.1.call-start = ((), (), s32[]{:S(2)}) async-start(), calls=%async_computation.17 | async-start | bytes 2162688 | tf_op jit(solution)/shard_map/all_gather | solution.py:19
  10.2 210.9 %all-gather.15.cloned.1.call-start = ((), (), s32[]{:S(2)}) async-start(), calls=%async_computation.12 | async-start | bytes 4325376 | tf_op jit(solution)/shard_map/all_gather | solution.py:129
  11.6 129.7 %copy-start.19 = (pred[4]{0:T(512)(128)(4,1)}, pred[4]{0:T(512)(128)(4,1)S(1)}, u32[]{:S(2)}) copy-start(pred[4]{0:T(512)(128)(4,1)S(1)} %get-tuple-element.37) | copy-start | bytes 16
  26.9 102.2 %all-to-all-start.1 = ((bf16[4,2,128,896]{3,2,1,0:T(8,128)(2,1)}), bf16[4,2,128,896]{3,2,1,0:T(8,128)(2,1)S(1)}, u32[]{:S(2)}, u32[]{:S(2)}) async-start(bf16[4,2,128,896]{3,2,1,0:T(8,128)(2,1)} %broadcast_select_fusion), calls=%async_computation.1 | async-start | bytes 3670016 | tf_op jit(solution)/shard_map/all_to_all | solution.py:154
  83.1 58.1 %copy-start.13 = (f32[896]{0:T(1024)S(1)}, f32[896]{0:T(1024)}, u32[]{:S(2)}) copy-start(f32[896]{0:T(1024)} %param.18) | copy-start | bytes 10756
  129.2 5.0 copy-start.4
  129.8 9.7 %all-to-all-start.2 = ((bf16[4,8,224]{2,1,0:T(8,128)(2,1)}), bf16[4,8,224]{2,1,0:T(8,128)(2,1)S(1)}, u32[]{:S(2)}, u32[]{:S(2)}) async-start(bf16[4,8,224]{2,1,0:T(8,128)(2,1)} %broadcast_in_dim.82), calls=%async_computation.2 | async-start | bytes 32768 | tf_op jit(solution)/shard_map/all_to_all | solution.py:30
  134.1 132.3 %all-gather.13.cloned.1.call-start = ((), (), s32[]{:S(2)}) async-start(), calls=%async_computation.11 | async-start | bytes 4587520 | tf_op jit(solution)/shard_map/all_gather | solution.py:167
  141.3 35.7 %copy-start.15 = (f32[4,128]{1,0:T(4,128)}, f32[4,128]{1,0:T(4,128)S(1)}, u32[]{:S(2)}) copy-start(f32[4,128]{1,0:T(4,128)S(1)} %get-tuple-element.46) | copy-start | bytes 6148
  142.6 173.8 %all-gather.19.cloned.1.call-start = ((), (), s32[]{:S(2)}) async-start(), calls=%async_computation.14 | async-start | bytes 5242880 | tf_op jit(solution)/shard_map/all_gather | solution.py:192
  143.2 225.1 %all-gather.17.cloned.1.call-start = ((), (), s32[]{:S(2)}) async-start(), calls=%async_computation.13 | async-start | bytes 4325376 | tf_op jit(solution)/shard_map/all_gather | solution.py:134
  144.0 440.3 %reduce-scatter.10.cloned.1.call-start = ((), (), s32[]{:S(2)}) async-start(), calls=%async_computation.18 | async-start | bytes 4325376
  177.0 44.1 %copy-start.17 = (f32[4096]{0:T(1024)S(1)}, f32[4096]{0:T(1024)}, u32[]{:S(2)}) copy-start(f32[4096]{0:T(1024)} %param.12) | copy-start | bytes 49156
  180.6 215.2 %copy-start.22 = (f32[512]{0:T(512)}, f32[512]{0:T(512)S(1)}, u32[]{:S(2)}) copy-start(f32[512]{0:T(512)S(1)} %get-tuple-element.44) | copy-start | bytes 6148
  289.4 2.0 copy-start.2
  329.5 256.6 %reduce-scatter.6.cloned.1.call-start = ((), (), s32[]{:S(2)}) async-start(), calls=%async_computation.15 | async-start | bytes 4325376 | tf_op jit(solution)/shard_map/reduce_scatter | solution.py:224
  434.2 1.6 copy-start.5
  434.2 2.9 copy-start.9
  434.9 4.6 copy-start.7
  443.9 48.9 %all-to-all-start.4 = ((bf16[4,512,896]{2,1,0:T(8,128)(2,1)}), bf16[4,512,896]{2,1,0:T(8,128)(2,1)}, u32[]{:S(2)}, u32[]{:S(2)}) async-start(bf16[4,512,896]{2,1,0:T(8,128)(2,1)} %bitcast.88), calls=%async_computation.4 | async-start | bytes 7340032 | tf_op jit(solution)/shard_map/all_to_all | solution.py:45
  448.9 6.7 copy-start.8
  448.9 6.7 copy-start.25
  455.7 3.0 copy-start.6
  461.7 34.2 %copy-start.14 = (f32[896]{0:T(1024)S(1)}, f32[896]{0:T(1024)}, u32[]{:S(2)}) copy-start(f32[896]{0:T(1024)} %param.18) | copy-start | bytes 10756
  461.7 34.2 %copy-start.20 = (pred[4]{0:T(512)(128)(4,1)S(1)}, pred[4]{0:T(512)(128)(4,1)}, u32[]{:S(2)}) copy-start(pred[4]{0:T(512)(128)(4,1)} %copy-done.19) | copy-start | bytes 16
  461.7 34.7 %copy-start.16 = (f32[4,128]{1,0:T(4,128)S(1)}, f32[4,128]{1,0:T(4,128)}, u32[]{:S(2)}) copy-start(f32[4,128]{1,0:T(4,128)} %copy-done.15) | copy-start | bytes 6148
  461.8 34.7 %copy-start.24 = (f32[4,128]{1,0:T(4,128)S(1)}, f32[4,128]{1,0:T(4,128)}, u32[]{:S(2)}) copy-start(f32[4,128]{1,0:T(4,128)} %get-tuple-element.45) | copy-start | bytes 6148
  497.9 13.9 %all-to-all-start.5 = ((f32[4,4,896]{2,1,0:T(4,128)}), f32[4,4,896]{2,1,0:T(4,128)S(1)}, u32[]{:S(2)}, u32[]{:S(2)}) async-start(f32[4,4,896]{2,1,0:T(4,128)} %broadcast_in_dim.84), calls=%async_computation.5 | async-start | bytes 114688 | tf_op jit(solution)/shard_map/all_to_all | solution.py:30
  506.2 2.4 copy-start.11
  508.6 1.2 copy-start.10
  511.8 67.6 %all-to-all-start.3 = ((bf16[4,512,1024]{2,1,0:T(8,128)(2,1)}), bf16[4,512,1024]{2,1,0:T(8,128)(2,1)}, u32[]{:S(2)}, u32[]{:S(2)}) async-start(bf16[4,512,1024]{2,1,0:T(8,128)(2,1)} %bitcast.80), calls=%async_computation.3 | async-start | bytes 8388608 | tf_op jit(solution)/shard_map/all_to_all | solution.py:45
  516.7 129.2 %all-reduce.3.cloned.1.call-start = ((), (), s32[]{:S(2)}) async-start(), calls=%async_computation.19 | async-start | bytes 8519680 | tf_op jit(solution)/shard_map/psum | solution.py:263
  527.7 203.4 %reduce-scatter.8.cloned.1.call-start = ((), (), s32[]{:S(2)}) async-start(), calls=%async_computation.16 | async-start | bytes 3784704 | tf_op jit(solution)/shard_map/reduce_scatter | solution.py:55
  542.8 40.1 %copy-start.3 = (bf16[512,1024]{1,0:T(8,128)(2,1)S(1)}, bf16[512,1024]{1,0:T(8,128)(2,1)}, u32[]{:S(2)}) copy-start(bf16[512,1024]{1,0:T(8,128)(2,1)} %param.11) | copy-start | bytes 3145732
  582.9 63.0 %copy-start.18 = (f32[4096]{0:T(1024)S(1)}, f32[4096]{0:T(1024)}, u32[]{:S(2)}) copy-start(f32[4096]{0:T(1024)} %param.12) | copy-start | bytes 49156
  645.9 4.9 copy-start.12
  650.9 1.0 copy-start.21
  650.9 1.0 copy-start.23
  651.9 83.0 %copy-start.1 = (bf16[8,128,896]{2,1,0:T(8,128)(2,1)S(1)}, bf16[8,128,896]{2,1,0:T(8,128)(2,1)}, u32[]{:S(2)}) copy-start(bf16[8,128,896]{2,1,0:T(8,128)(2,1)} %param.19) | copy-start | bytes 5505028
Sparse Core Ops, SparseCore 0:
  9.7 70.3 all-gather.8
  82.3 44.7 all-gather.10
  129.9 43.2 all-gather.20
  175.4 45.6 all-gather.14
  223.1 43.2 all-gather.12
  267.9 48.4 all-gather.18
  318.6 49.7 all-gather.16
  372.0 81.5 reduce-scatter.9
  457.7 81.2 reduce-scatter.5
  541.9 103.9 all-reduce.2
  650.0 81.0 reduce-scatter.7
where the time goes:
time: 752 us; the launch traced here: 742 us
  waiting for transfers between devices  467 us (62%)
  matrix products  119 us (16%)
  local copies, waits for them, and re-layouts  60.3 us (8%)
  other arithmetic  48.4 us (6%)
  starting transfers between devices  22.4 us (3%)
  between operations  14.9 us (2%)
  blocking collectives  9.59 us (1%)
    reduce_scatter x1, waiting for transfers between devices, one_scatter(): lax.psum_scatter(lines, axis, tiled=True).reshape(-1)  75.2 us
    all_to_all x2, waiting for transfers between devices, summed_on_arrival(): tiles = lax.all_to_all(in_blocks(shard, dim, peers), axis, 0, 0, tiled=True)  67.6 us
    psum x1, waiting for transfers between devices, shards(): lax.psum(summary_term.astype(jnp.bfloat16), 'enc').astype(jnp.float32)  58.2 us
    all_gather x1, waiting for transfers between devices, shards(): full_rows = lax.all_gather(hidden, 'enc', axis=1, tiled=True)  49.5 us
    all_gather x1, waiting for transfers between devices, shards(): lax.all_gather(w_cond, 'dp', axis=0, tiled=True)  43.9 us
    all_gather x1, waiting for transfers between devices, shards(): lax.all_gather(w_query, 'dp', axis=0, tiled=True)  40.4 us
    all_gather x1, waiting for transfers between devices, shards(): encoded = lax.all_gather(encoded_mine, 'enc', axis=0, tiled=True)  39.4 us
    all_gather x1, waiting for transfers between devices, shards(): w_out_all = lax.all_gather(w_out, 'dp', axis=1, tiled=True)  38.4 us
  transfers between devices with their start and end apart: 16, of which 12 were waited for; matrix products, arithmetic and copies ran while one was open for 30% of the time, Pallas kernels for 0%

commit v1 on v0

--- a/solution.py
+++ b/solution.py
@@ -260,7 +260,9 @@
     normed_term = contract_last(query_act_grad, w_query_all)
     normed_grad, summary_grad = (
         lax.psum(normed_term.astype(jnp.bfloat16), "enc").astype(jnp.float32),
-        lax.psum(summary_term.astype(jnp.bfloat16), "enc").astype(jnp.float32),
+        jnp.sum(lax.all_gather(summary_term.astype(jnp.bfloat16), "enc"), axis=0).astype(
+            jnp.float32
+        ),
     )
     scaled = normed_grad * norm_gain
     row_mean = jnp.mean(inputs * scaled, axis=-1, keepdims=True)

time: 752 us -> 816 us (1.085)
  blocking collectives: 9.59 us -> 57.7 us
  waiting for transfers between devices: 467 us -> 490 us
    psum x1, waiting for transfers between devices: 58.2 us -> 0.01 us  [shards(): lax.psum(normed_term.astype(jnp.bfloat16), 'enc').astype(jnp.float32)]
    all_gather x0 -> x1, blocking collectives: none -> 48.1 us  [shards(): lax.all_gather(summary_term.astype(jnp.bfloat16), 'enc')]
    reduce_scatter x1, waiting for transfers between devices: 0.01 us -> 47.3 us  [shards(): lax.psum_scatter(contract_first(normed, query_act_grad).astype(jnp.bfloat...]
    all_gather x1, waiting for transfers between devices: 18.7 us -> 43.1 us  [shards(): grad_rows = lax.all_gather(out_grad, 'enc', axis=1, tiled=True)]
    all_to_all x2, waiting for transfers between devices: 67.6 us -> 54.1 us  [summed_on_arrival(): tiles = lax.all_to_all(in_blocks(shard, dim, peers), axis, 0, 0, tiled=True)]
    all_gather x1, waiting for transfers between devices: 38.4 us -> 51.8 us  [shards(): w_out_all = lax.all_gather(w_out, 'dp', axis=1, tiled=True)]
    unnamed x58 -> x44, local copies, waits for them, and re-layouts: 17.1 us -> 18.5 us
  transfers between devices with their start and end apart: 16 -> 16, of which waited for: 12 -> 11; matrix products, arithmetic and copies ran while one was open for 30% -> 21% of each run, Pallas kernels for 0% -> 0%
where the time goes in v1:
time: 816 us; the launch traced here: 810 us
  waiting for transfers between devices  490 us (60%)
  matrix products  116 us (14%)
  local copies, waits for them, and re-layouts  62.9 us (8%)
  blocking collectives  57.7 us (7%)
  other arithmetic  47.1 us (6%)
  starting transfers between devices  21.9 us (3%)
  between operations  14.5 us (2%)
    reduce_scatter x1, waiting for transfers between devices, one_scatter(): lax.psum_scatter(lines, axis, tiled=True).reshape(-1)  83 us
    all_to_all x2, waiting for transfers between devices, summed_on_arrival(): tiles = lax.all_to_all(in_blocks(shard, dim, peers), axis, 0, 0, tiled=True)  54.1 us
    all_gather x1, waiting for transfers between devices, shards(): w_out_all = lax.all_gather(w_out, 'dp', axis=1, tiled=True)  51.8 us
    all_gather x1, waiting for transfers between devices, shards(): full_rows = lax.all_gather(hidden, 'enc', axis=1, tiled=True)  49.1 us
    all_gather x1, blocking collectives, shards(): lax.all_gather(summary_term.astype(jnp.bfloat16), 'enc')  48.1 us
    reduce_scatter x1, waiting for transfers between devices, shards(): lax.psum_scatter(contract_first(normed, query_act_grad).astype(jnp.bfloat...  47.3 us
    all_gather x1, waiting for transfers between devices, shards(): lax.all_gather(w_cond, 'dp', axis=0, tiled=True)  43.9 us
    all_gather x1, waiting for transfers between devices, shards(): grad_rows = lax.all_gather(out_grad, 'enc', axis=1, tiled=True)  43.1 us
  transfers between devices with their start and end apart: 16, of which 11 were waited for; matrix products, arithmetic and copies ran while one was open for 21% of the time, Pallas kernels for 0%

profile of v1, /device:TPU:0, one launch (start us, length us, event | category | flops | bytes accessed | tf_op | source)
XLA Modules:
  0.0 810.5 jit_solution(6479084069623310542)
XLA Ops:
  12.3 9.6 %all_to_all.40 = s32[4,1,2]{2,1,0:T(1,128)S(1)} all-to-all(s32[4,1,2]{2,1,0:T(1,128)S(1)} %bitcast.101), channel_id=1, replica_groups=mesh['dp'=32,'enc'=4] {'enc'}, dimensions={0} | all-to-all | bytes 64 | tf_op jit(solution)/shard_map/all_to_all | solution.py:157
  24.3 3.0 broadcast_select_fusion
  27.3 3.6 all-to-all-start.1
  31.0 49.1 %all-gather.10.cloned.1.call-done = bf16[512,4096]{1,0:T(8,128)(2,1)} async-done(((bf16[512,1024]{1,0:T(8,128)(2,1)}), bf16[512,4096]{1,0:T(8,128)(2,1)}) %all-gather.10.cloned.1.call-update) | async-done | bytes 4194320 | tf_op jit(solution)/shard_map/all_gather | solution.py:124
  80.1 3.0 bitcast_reduce_fusion
  83.2 43.9 %all-gather.12.cloned.1.call-done = bf16[4096,224]{0,1:T(8,128)(2,1)} async-done(((bf16[128,224]{0,1:T(8,128)(2,1)}), bf16[4096,224]{0,1:T(8,128)(2,1)}) %all-gather.12.cloned.1.call-update) | async-done | bytes 1835024 | tf_op jit(solution)/shard_map/all_gather | solution.py:131
  129.8 4.3 all-to-all-start.2
  136.4 3.1 all-to-all-done.2
  142.4 30.8 %all-gather.22.cloned.1.call-done = bf16[32,28,1024]{2,1,0:T(8,128)(2,1)} async-done(((bf16[1,28,1024]{2,1,0:T(8,128)(2,1)}), bf16[32,28,1024]{2,1,0:T(8,128)(2,1)}) %all-gather.22.cloned.1.call-update) | async-done | bytes 1835024 | tf_op jit(solution)/shard_map/all_gather | solution.py:19
  173.3 3.7 reshape.331
  177.0 3.1 multiply_reduce_fusion.1
  180.1 41.0 %all-gather.16.cloned.1.call-done = bf16[4096,512]{1,0:T(8,128)(2,1)} async-done(((bf16[128,512]{1,0:T(8,128)(2,1)}), bf16[4096,512]{1,0:T(8,128)(2,1)}) %all-gather.16.cloned.1.call-update) | async-done | bytes 4194320 | tf_op jit(solution)/shard_map/all_gather | solution.py:129
  221.1 5.8 convolution_convert_fusion.11
  227.0 43.1 %all-gather.20.cloned.1.call-done = bf16[512,4096]{1,0:T(8,128)(2,1)} async-done(((bf16[512,1024]{1,0:T(8,128)(2,1)}), bf16[512,4096]{1,0:T(8,128)(2,1)}) %all-gather.20.cloned.1.call-update) | async-done | bytes 4194320 | tf_op jit(solution)/shard_map/all_gather | solution.py:192
  270.1 51.8 %all-gather.18.cloned.1.call-done = bf16[512,4096]{1,0:T(8,128)(2,1)} async-done(((bf16[512,128]{1,0:T(8,128)(2,1)}), bf16[512,4096]{1,0:T(8,128)(2,1)}) %all-gather.18.cloned.1.call-update) | async-done | bytes 4194320 | tf_op jit(solution)/shard_map/all_gather | solution.py:134
  321.9 5.8 convolution_convert_fusion.10
  327.9 39.7 %all-gather.14.cloned.1.call-done = bf16[16,128,896]{2,1,0:T(8,128)(2,1)} async-done(((bf16[4,128,896]{2,1,0:T(8,128)(2,1)}), bf16[16,128,896]{2,1,0:T(8,128)(2,1)}) %all-gather.14.cloned.1.call-update) | async-done | bytes 3670032 | tf_op jit(solution)/shard_map/all_gather | solution.py:167
  367.6 6.1 convolution_convert_fusion.6
  373.7 3.7 convolution_convert_fusion.7
  377.4 4.0 reshape.289
  381.4 4.5 reshape.287
  393.6 16.1 %fusion.37 = bf16[8,64,4,128]{3,1,2,0:T(8,128)(2,1)} fusion(bf16[8,256,4,128]{3,2,1,0:T(4,128)(2,1)} %reshape.289, f32[8,4,64,256]{3,2,1,0:T(8,128)} %fusion.9, f32[8,4,64,256]{3,2,1,0:T(8,128)} %get-tuple-element.48, f32[8,4,64]{2,1,0:T(4,128)S(1)} %get-tuple-element.47), kind=kOutput, calls=%fused_computation.62 | convolution fusion | flops 138152192 | bytes 6823936 | tf_op jit(solution)/shard_map/chqk,ckhd->cqhd/dot_general | solution.py:210
  411.1 6.7 convolution_convert_fusion.2
  417.9 6.7 fusion.34
  426.0 7.0 convolution_convert_fusion
  433.0 6.6 copy.112
  439.7 16.6 %convert_bitcast_fusion.1 = bf16[8,256,4,128]{1,3,2,0:T(8,128)(2,1)} fusion(f32[8,4,64,256]{3,2,1,0:T(8,128)} %fusion.9, bf16[8,64,4,128]{3,2,1,0:T(4,128)(2,1)S(1)} %reshape.288, f32[8,4,64,256]{3,2,1,0:T(8,128)} %get-tuple-element.48, f32[8,4,64]{2,1,0:T(4,128)S(1)} %get-tuple-element.47), kind=kOutput, calls=%fused_computation.29 | convolution fusion | flops 138938624 | bytes 6823936 | tf_op jit(solution)/shard_map/chqk,cqhd->ckhd/dot_general | solution.py:215
  461.1 7.0 convert_bitcast_fusion
  476.5 4.4 add_convert_fusion
  480.9 4.7 all-to-all-start.4
  485.7 6.0 convolution_convert_fusion.8
  491.7 4.6 convolution_convert_fusion.1
  496.2 54.1 %all-to-all-done.4 = bf16[4,512,896]{2,1,0:T(8,128)(2,1)} async-done(((bf16[4,512,896]{2,1,0:T(8,128)(2,1)}), bf16[4,512,896]{2,1,0:T(8,128)(2,1)}, u32[]{:S(2)}, u32[]{:S(2)}) %all-to-all-start.4) | async-done | bytes 3670048 | tf_op jit(solution)/shard_map/all_to_all | solution.py:45
  550.3 3.1 reduce_sum.145
  555.4 3.3 all-to-all-start.5
  559.1 5.0 convolution_convert_fusion.9
  570.7 5.0 reshape_reshape.15
  575.8 3.0 pad_maximum_fusion
  578.8 5.2 reshape.298
  584.0 4.5 convolution_convert_fusion.3
  591.0 4.8 all-to-all-start.3
  595.9 6.6 convert_element_type.165
  602.9 48.1 %all-gather = bf16[32,4096]{1,0:T(8,128)(2,1)S(1)} all-gather(bf16[8,4096]{1,0:T(8,128)(2,1)S(1)} %convolution_convert_fusion.5), channel_id=2, replica_groups=mesh['dp'=32,'enc'=4] {'enc'}, dimensions={0}, use_global_device_ids=true | all-gather | bytes 327680 | tf_op jit(solution)/shard_map/all_gather | solution.py:263
  651.0 3.6 convert_reduce_fusion
  656.0 5.2 multiply_reduce_fusion
  662.2 4.1 dynamic-slice_add_fusion
  668.1 47.3 %reduce-scatter.6.cloned.1.call-done = bf16[128,512]{1,0:T(8,128)(2,1)} async-done(((bf16[4096,512]{1,0:T(8,128)(2,1)}), bf16[128,512]{1,0:T(8,128)(2,1)}) %reduce-scatter.6.cloned.1.call-update) | async-done | bytes 131088 | tf_op jit(solution)/shard_map/reduce_scatter | solution.py:224
  717.0 83.0 %reduce-scatter.8.cloned.1.call-done = bf16[448,128]{1,0:T(8,128)(2,1)} async-done(((bf16[14336,128]{1,0:T(8,128)(2,1)}), bf16[448,128]{1,0:T(8,128)(2,1)}) %reduce-scatter.8.cloned.1.call-update) | async-done | bytes 114704 | tf_op jit(solution)/shard_map/reduce_scatter | solution.py:55
  (133 shorter events, 60.7 us)
Async XLA Ops:
  7.2 15.1 %copy-start = (bf16[8,128,896]{2,1,0:T(8,128)(2,1)S(1)}, bf16[8,128,896]{2,1,0:T(8,128)(2,1)}, u32[]{:S(2)}) copy-start(bf16[8,128,896]{2,1,0:T(8,128)(2,1)} %param.19) | copy-start | bytes 5505028
  7.2 4.7 copy-start.18
  7.2 72.9 %all-gather.10.cloned.1.call-start = ((), (), s32[]{:S(2)}) async-start(), calls=%async_computation.9 | async-start | bytes 5242880 | tf_op jit(solution)/shard_map/all_gather | solution.py:124
  7.9 119.2 %all-gather.12.cloned.1.call-start = ((), (), s32[]{:S(2)}) async-start(), calls=%async_computation.10 | async-start | bytes 1892352 | tf_op jit(solution)/shard_map/all_gather | solution.py:131
  8.7 164.6 %all-gather.22.cloned.1.call-start = ((), (), s32[]{:S(2)}) async-start(), calls=%async_computation.18 | async-start | bytes 2162688 | tf_op jit(solution)/shard_map/all_gather | solution.py:19
  10.2 210.9 %all-gather.16.cloned.1.call-start = ((), (), s32[]{:S(2)}) async-start(), calls=%async_computation.12 | async-start | bytes 4325376 | tf_op jit(solution)/shard_map/all_gather | solution.py:129
  10.7 259.4 %all-gather.20.cloned.1.call-start = ((), (), s32[]{:S(2)}) async-start(), calls=%async_computation.14 | async-start | bytes 5242880 | tf_op jit(solution)/shard_map/all_gather | solution.py:192
  11.3 310.6 %all-gather.18.cloned.1.call-start = ((), (), s32[]{:S(2)}) async-start(), calls=%async_computation.13 | async-start | bytes 4325376 | tf_op jit(solution)/shard_map/all_gather | solution.py:134
  27.3 101.8 %all-to-all-start.1 = ((bf16[4,2,128,896]{3,2,1,0:T(8,128)(2,1)}), bf16[4,2,128,896]{3,2,1,0:T(8,128)(2,1)S(1)}, u32[]{:S(2)}, u32[]{:S(2)}) async-start(bf16[4,2,128,896]{3,2,1,0:T(8,128)(2,1)} %broadcast_select_fusion), calls=%async_computation.1 | async-start | bytes 3670016 | tf_op jit(solution)/shard_map/all_to_all | solution.py:154
  83.1 57.6 %copy-start.15 = (f32[896]{0:T(1024)S(1)}, f32[896]{0:T(1024)}, u32[]{:S(2)}) copy-start(f32[896]{0:T(1024)} %param.18) | copy-start | bytes 10756
  129.2 5.0 copy-start.7
  129.8 9.7 %all-to-all-start.2 = ((bf16[4,8,224]{2,1,0:T(8,128)(2,1)}), bf16[4,8,224]{2,1,0:T(8,128)(2,1)S(1)}, u32[]{:S(2)}, u32[]{:S(2)}) async-start(bf16[4,8,224]{2,1,0:T(8,128)(2,1)} %broadcast_in_dim.82), calls=%async_computation.2 | async-start | bytes 32768 | tf_op jit(solution)/shard_map/all_to_all | solution.py:30
  134.1 233.4 %all-gather.14.cloned.1.call-start = ((), (), s32[]{:S(2)}) async-start(), calls=%async_computation.11 | async-start | bytes 4587520 | tf_op jit(solution)/shard_map/all_gather | solution.py:167
  142.1 514.0 %all-reduce.2.cloned.1.call-start = ((), (), s32[]{:S(2)}) async-start(), calls=%async_computation.15 | async-start | bytes 8388608 | tf_op jit(solution)/shard_map/psum | solution.py:262
  177.0 44.1 %copy-start.16 = (f32[4096]{0:T(1024)S(1)}, f32[4096]{0:T(1024)}, u32[]{:S(2)}) copy-start(f32[4096]{0:T(1024)} %param.12) | copy-start | bytes 49156
  367.6 6.1 copy-start.10
  367.6 6.1 copy-start.17
  388.3 2.1 copy-start.3
  388.3 3.1 copy-start.4
  411.1 6.7 copy-start.13
  417.9 248.5 %reduce-scatter.10.cloned.1.call-start = ((), (), s32[]{:S(2)}) async-start(), calls=%async_computation.19 | async-start | bytes 4325376
  470.9 1.6 copy-start.8
  470.9 3.0 copy-start.11
  471.6 5.0 copy-start.9
  480.9 69.4 %all-to-all-start.4 = ((bf16[4,512,896]{2,1,0:T(8,128)(2,1)}), bf16[4,512,896]{2,1,0:T(8,128)(2,1)}, u32[]{:S(2)}, u32[]{:S(2)}) async-start(bf16[4,512,896]{2,1,0:T(8,128)(2,1)} %bitcast.90), calls=%async_computation.4 | async-start | bytes 7340032 | tf_op jit(solution)/shard_map/all_to_all | solution.py:45
  485.7 6.0 copy-start.2
  485.7 6.0 copy-start.14
  555.4 12.0 %all-to-all-start.5 = ((f32[4,4,896]{2,1,0:T(4,128)}), f32[4,4,896]{2,1,0:T(4,128)S(1)}, u32[]{:S(2)}, u32[]{:S(2)}) async-start(f32[4,4,896]{2,1,0:T(4,128)} %broadcast_in_dim.84), calls=%async_computation.5 | async-start | bytes 114688 | tf_op jit(solution)/shard_map/all_to_all | solution.py:30
  558.7 156.7 %reduce-scatter.6.cloned.1.call-start = ((), (), s32[]{:S(2)}) async-start(), calls=%async_computation.16 | async-start | bytes 4325376 | tf_op jit(solution)/shard_map/reduce_scatter | solution.py:224
  564.1 1.2 copy-start.12
  567.3 232.7 %reduce-scatter.8.cloned.1.call-start = ((), (), s32[]{:S(2)}) async-start(), calls=%async_computation.17 | async-start | bytes 3784704 | tf_op jit(solution)/shard_map/reduce_scatter | solution.py:55
  591.0 60.0 %all-to-all-start.3 = ((bf16[4,512,1024]{2,1,0:T(8,128)(2,1)}), bf16[4,512,1024]{2,1,0:T(8,128)(2,1)}, u32[]{:S(2)}, u32[]{:S(2)}) async-start(bf16[4,512,1024]{2,1,0:T(8,128)(2,1)} %bitcast.82), calls=%async_computation.3 | async-start | bytes 8388608 | tf_op jit(solution)/shard_map/all_to_all | solution.py:45
  595.8 6.6 copy-start.5
  651.0 3.7 copy-start.6
  662.2 141.5 %copy-start.1 = (bf16[8,128,896]{2,1,0:T(8,128)(2,1)S(1)}, bf16[8,128,896]{2,1,0:T(8,128)(2,1)}, u32[]{:S(2)}) copy-start(bf16[8,128,896]{2,1,0:T(8,128)(2,1)} %param.19) | copy-start | bytes 5505028
Sparse Core Ops, SparseCore 0:
  9.7 70.3 all-gather.9
  82.3 44.7 all-gather.11
  129.9 43.2 all-gather.21
  175.4 45.6 all-gather.15
  222.6 47.5 all-gather.19
  272.2 49.7 all-gather.17
  324.2 43.3 all-gather.13
  418.0 113.4 all-reduce.1
  535.6 94.9 reduce-scatter.9
  634.1 81.2 reduce-scatter.5
  719.5 80.5 reduce-scatter.7
